TPU v7x, 256 devices: a whole 4x4x8 slice. The times are simulated.
256 devices in a mesh: ctx: 32 (over z_hi, x, core), tp: 8 (over y, z_lo).
Axes of the slice: x: 4, y: 4, z: 8 (z_hi: 4, z_lo: 2; z = z_hi * 2 + z_lo), core: 2. Of those that a mesh axis runs over, the one named last changes fastest.
Arguments:
- features: bfloat16 [16384, 3, 4096], P('ctx', None, 'tp'), may hold values from -6 to 6
- short_filter: float32 [3, 7, 4096], P(None, None, 'tp'), may hold values from -2 to 2
- decay_rate: float32 [16, 4096], P(None, 'tp'), may hold values from 0 to 1, as said below
- residue: float32 [16, 4096], P(None, 'tp'), may hold values from -2 to 2
- skip_gain: float32 [4096], P('tp'), may hold values from -4 to 4
- norm_gain: float32 [4096], replicated, may hold values from 0.1 to 1.9
- qkv_weight: bfloat16 [4096, 3, 2048], P('ctx', None, 'tp'), may hold values from -2 to 2
Outputs:
- mixer: bfloat16 [16384, 4096], P('ctx', 'tp')
- attended: bfloat16 [16384, 2048], P('ctx', 'tp')
Inputs may be any that keep to these rules, and one draw needn't show every extreme that they name: `decay_rate`: decay rates are positive.
All inputs are finite; a program needn't handle non-finite values.
Results may differ from a plain program's by a relative error of at most 0.01.
Values may be sent and summed in bfloat16 or wider, within the bound.
No kernel may reach another device: no remote copies, remote signals or barrier semaphores. Data moves between devices by JAX's collectives and lax.ppermute only.
A program may use at most 128 MiB of HBM per device.

v0:
```python
from functools import reduce
import math
import jax
import jax.numpy as jnp
from jax import lax
from jax.sharding import PartitionSpec as P

HD = 128
TAPS = 7
WINDOW = 3
CHUNK = 128
EPSILON = 1e-06
PRECISE = lax.Precision.HIGHEST


def to_bf16_grid(value):
    return lax.reduce_precision(value, exponent_bits=8, mantissa_bits=7)


def from_behind(value, axis, steps):
    count = lax.axis_size(axis)
    leading, last = (max(0, -steps), min(count, count - steps))
    return lax.ppermute(value, axis, [(source, source + steps) for source in range(leading, last)])


def local_modal_conv(signal, decay, mixing):
    tokens, channels = signal.shape
    modes = decay.shape[0]
    chunks = tokens // CHUNK
    centre = (CHUNK - 1) / 2.0
    offsets = jnp.arange(CHUNK, dtype=jnp.float32) - centre
    up = jnp.exp(offsets[:, None, None] * decay[None])
    down = jnp.exp(-offsets[:, None, None] * decay[None])
    after = jnp.exp(-(jnp.arange(CHUNK, dtype=jnp.float32) + 1.0)[:, None, None] * decay[None])
    tri = (jnp.arange(CHUNK)[:, None] >= jnp.arange(CHUNK)[None, :]).astype(jnp.float32)
    blocks = signal.reshape(chunks, CHUNK, channels)
    lifted = (up[None] * blocks[:, :, None, :]).reshape(chunks, CHUNK, modes * channels)
    summed = jnp.einsum("ts,qsk->qtk", tri, lifted, precision=PRECISE).reshape(
        chunks, CHUNK, modes, channels
    )
    states = down[None] * summed
    intra = jnp.sum(states * mixing[None, None], axis=2)
    ends = states[:, CHUNK - 1]
    step = jnp.exp(-float(CHUNK) * decay)
    carry = jnp.zeros_like(decay)
    entering = []
    for chunk in range(chunks):
        entering.append(carry)
        carry = step * carry + ends[chunk]
    entering = jnp.stack(entering)
    weighted_after = after * mixing[None]
    return (intra, entering, carry, weighted_after)


def on_device(features, short_filter, decay_rate, residue, skip_gain, norm_gain, qkv_weight):
    tok_dev, _, channels = features.shape
    head_cols = qkv_weight.shape[2]
    shard_rows = lax.all_gather(qkv_weight, "ctx", axis=0, tiled=True)
    rim_rows = features[tok_dev - (TAPS - 1) :]
    before = from_behind(rim_rows, "ctx", 1)
    extended = jnp.concatenate([before, features], axis=0).astype(jnp.float32)
    short_conv = jnp.zeros((tok_dev, 3, channels), jnp.float32)
    for offset in range(TAPS):
        first_row = TAPS - 1 - offset
        short_conv = (
            short_conv
            + short_filter[:, offset, :][None] * extended[first_row : first_row + tok_dev]
        )
    gated = to_bf16_grid(short_conv[:, 1] * short_conv[:, 2])
    mixing = residue * jnp.sqrt(decay_rate)
    intra, entering, block_end, weighted_after = local_modal_conv(gated, decay_rate, mixing)
    block_step = jnp.exp(-float(tok_dev) * decay_rate)
    history = from_behind(block_end, "ctx", 1)
    factor = block_step
    count = lax.axis_size("ctx")
    shift = 1
    while shift < count:
        history = history + factor * from_behind(history, "ctx", shift)
        factor = factor * factor
        shift *= 2
    chunks = tok_dev // CHUNK
    chunk_step = jnp.exp(-float(CHUNK) * decay_rate)
    lead = [jnp.ones_like(decay_rate)]
    for chunk in range(1, chunks):
        lead.append(lead[-1] * chunk_step)
    lead = jnp.stack(lead)
    total_state = entering + lead * history[None]
    carried = jnp.einsum("lnc,qnc->qlc", weighted_after, total_state, precision=PRECISE)
    filtered = (intra + carried).reshape(tok_dev, channels) + skip_gain[None] * gated
    filtered = to_bf16_grid(filtered)
    mixer = (short_conv[:, 0] * filtered).astype(jnp.bfloat16)
    gathered = lax.all_gather(mixer, "tp", axis=1, tiled=True)
    as_float = gathered.astype(jnp.float32)
    inverse = lax.rsqrt(jnp.mean(as_float * as_float, axis=1, keepdims=True) + EPSILON)
    normed = (as_float * inverse * norm_gain[None]).astype(jnp.bfloat16)
    flat_rows = shard_rows.reshape(shard_rows.shape[0], 3 * head_cols)
    projected = jnp.dot(normed, flat_rows, preferred_element_type=jnp.float32).astype(jnp.bfloat16)
    heads = head_cols // HD
    query = projected[:, :head_cols].reshape(tok_dev, heads, HD)
    kv_pair = projected[:, head_cols:]
    blocks_kv = [kv_pair] + [from_behind(kv_pair, "ctx", lag) for lag in range(1, WINDOW)]
    position = lax.axis_index("ctx")
    row_ids = jnp.arange(tok_dev)
    causal = row_ids[:, None] >= row_ids[None, :]
    score_list = []
    for lag_step in range(WINDOW):
        keys = blocks_kv[lag_step][:, :head_cols].reshape(tok_dev, heads, HD)
        scores = jnp.einsum(
            "thd,shd->hts", query, keys, preferred_element_type=jnp.float32
        ) / math.sqrt(HD)
        if lag_step == 0:
            allowed = causal
        else:
            allowed = jnp.broadcast_to(position >= lag_step, causal.shape)
        score_list.append(jnp.where(allowed[None], scores, -jnp.inf))
    peak = reduce(jnp.maximum, [jnp.max(entry, axis=2) for entry in score_list])
    total = jnp.zeros((heads, tok_dev), jnp.float32)
    output = jnp.zeros((tok_dev, heads, HD), jnp.float32)
    for lag_step in range(WINDOW):
        expo = jnp.exp(score_list[lag_step] - peak[:, :, None])
        total = total + jnp.sum(expo, axis=2)
        values = blocks_kv[lag_step][:, head_cols:].reshape(tok_dev, heads, HD)
        output = output + jnp.einsum(
            "hts,shd->thd", expo.astype(jnp.bfloat16), values, preferred_element_type=jnp.float32
        )
    attended = (output / total.T[:, :, None]).astype(jnp.bfloat16).reshape(tok_dev, head_cols)
    return (mixer, attended)


def solution(mesh):
    placed = (
        P("ctx", None, "tp"),
        P(None, None, "tp"),
        P(None, "tp"),
        P(None, "tp"),
        P("tp"),
        P(),
        P("ctx", None, "tp"),
    )
    return jax.shard_map(
        on_device,
        mesh=mesh,
        in_specs=placed,
        out_specs=(P("ctx", "tp"), P("ctx", "tp")),
        check_vma=False,
    )
```

profile of v0, /device:TPU:105, one launch (start us, length us, event | category | flops | bytes accessed | tf_op | source)
XLA Modules:
  0.0 396.7 jit_solution(14588440854774348517)
XLA Ops:
  8.0 3.7 collective-permute-start
  15.3 4.6 %multiply_exponential_fusion = f32[128,8192]{0,1:T(8,128)} fusion(f32[8192]{0:T(1024)S(1)} %bitcast.158, f32[128]{0:T(128)S(1)} %iota_add_fusion), kind=kLoop, calls=%fused_computation.15 | loop fusion | flops 1048576 | bytes 4227584 | tf_op jit(solution)/shard_map/exp | solution.py:32
  19.9 3.6 multiply_exponential_fusion.1
  23.5 5.8 %copy.51 = f32[128,16,512]{2,1,0:T(8,128)} copy(f32[128,16,512]{0,1,2:T(8,128)} %multiply_exponential_fusion.1) | data formatting | bytes 8388608 | tf_op jit(solution)/shard_map/exp | solution.py:33
  36.1 9.5 %bitcast_multiply_fusion = f32[4,128,8192]{1,2,0:T(8,128)} fusion(f32[4,128,512]{1,2,0:T(8,128)} %copy.52, f32[128,8192]{0,1:T(8,128)} %multiply_exponential_fusion), kind=kLoop, calls=%fused_computation | loop fusion | flops 4194304 | bytes 22020096 | tf_op jit(solution)/shard_map/mul | solution.py:37
  45.6 14.5 %fusion.78 = f32[4,8192,128]{2,1,0:T(8,128)} fusion(f32[4,128,8192]{1,2,0:T(8,128)} %bitcast_multiply_fusion), kind=kOutput, calls=%fused_computation.102 | convolution fusion | flops 6442467328 | bytes 33554432 | tf_op jit(solution)/shard_map/ts,qsk->qtk/dot_general | solution.py:38
  60.1 19.9 %copy.53 = f32[4,128,16,512]{3,2,1,0:T(8,128)} copy(f32[4,128,16,512]{1,3,2,0:T(8,128)} %bitcast.151) | data formatting | bytes 33554432 | tf_op jit(solution)/shard_map/reshape | solution.py:38
  80.0 10.5 %multiply_reduce_fusion = (f32[4,128,512]{2,1,0:T(8,128)}, f32[4,128,16,512]{3,2,1,0:T(8,128)S(1)}) fusion(f32[16,512]{1,0:T(8,128)S(1)} %sqrt_multiply_fusion, f32[4,128,16,512]{3,2,1,0:T(8,128)} %copy.53, f32[128,16,512]{2,1,0:T(8,128)} %copy.51), kind=kLoop, calls=%fused_computation.1 | loop fusion | flops 12320768 | bytes 38830080 | tf_op jit(solution)/shard_map/reduce_sum | solution.py:42
  94.2 4.0 %collective-permute-start.2 = (f32[16,512]{1,0:T(8,128)S(1)}, f32[16,512]{1,0:T(8,128)S(1)}, u32[]{:S(2)}, u32[]{:S(2)}) collective-permute-start(f32[16,512]{1,0:T(8,128)S(1)} %collective-permute-done.1), channel_id=1, source_target_pairs={{0,8},{8,16},{16,24},{24,32},{32,40},{40,48},{48,56},{56,64},{64,7... | collective-permute-start | bytes 98312 | tf_op jit(solution)/shard_map/ppermute | solution.py:23
  98.3 2.6 collective-permute-done.2
  103.0 6.0 %collective-permute-done.3 = f32[16,512]{1,0:T(8,128)S(1)} collective-permute-done((f32[16,512]{1,0:T(8,128)S(1)}, f32[16,512]{1,0:T(8,128)S(1)}, u32[]{:S(2)}, u32[]{:S(2)}) %collective-permute-start.3) | collective-permute-done | bytes 32800 | tf_op jit(solution)/shard_map/ppermute | solution.py:23
  109.0 5.1 %collective-permute-start.4 = (f32[16,512]{1,0:T(8,128)S(1)}, f32[16,512]{1,0:T(8,128)S(1)}, u32[]{:S(2)}, u32[]{:S(2)}) collective-permute-start(f32[16,512]{1,0:T(8,128)S(1)} %multiply_add_fusion.3), channel_id=1, source_target_pairs={{0,32},{8,40},{16,48},{24,56},{32,64},{40,72},{48,80},{56,88},{64,... | collective-permute-start | bytes 98312 | tf_op jit(solution)/shard_map/ppermute | solution.py:23
  114.2 2.8 collective-permute-done.4
  117.0 8.7 %collective-permute-start.5 = (f32[16,512]{1,0:T(8,128)S(1)}, f32[16,512]{1,0:T(8,128)S(1)}, u32[]{:S(2)}, u32[]{:S(2)}) collective-permute-start(f32[16,512]{1,0:T(8,128)S(1)} %multiply_add_fusion.2), channel_id=1, source_target_pairs={{0,64},{8,72},{16,80},{24,88},{32,96},{40,104},{48,112},{56,120},{... | collective-permute-start | bytes 98312 | tf_op jit(solution)/shard_map/ppermute | solution.py:23
  126.8 4.9 %collective-permute-start.6 = (f32[16,512]{1,0:T(8,128)S(1)}, f32[16,512]{1,0:T(8,128)}, u32[]{:S(2)}, u32[]{:S(2)}) collective-permute-start(f32[16,512]{1,0:T(8,128)S(1)} %multiply_add_fusion.1), channel_id=1, source_target_pairs={{0,128},{8,136},{16,144},{24,152},{32,160},{40,168},{48,176},{56,1... | collective-permute-start | bytes 98312 | tf_op jit(solution)/shard_map/ppermute | solution.py:23
  139.6 7.4 %fusion.35 = f32[4,128,512]{1,0,2:T(4,128)} fusion(f32[4,128,512]{1,0,2:T(4,128)} %copy.56, f32[4,16,512]{1,0,2:T(4,128)} %copy.55, f32[16,512]{0,1:T(8,128)} %copy.54, f32[128]{0:T(128)S(1)} %add_negate_fusion, f32[16,512]{0,1:T(8,128)S(1)} %copy.50), kind=kOutput, calls=%fused_computation.51 | convolution fusion | flops 52690944 | bytes 2294272 | tf_op jit(solution)/shard_map/lnc,qnc->qlc/dot_general | solution.py:88
  153.2 102.1 %all-gather.3.cloned.1.call-done = bf16[512,4096]{1,0:T(8,128)(2,1)} async-done(((bf16[512,512]{1,0:T(8,128)(2,1)}), bf16[512,4096]{1,0:T(8,128)(2,1)}) %all-gather.3.cloned.1.call-update) | async-done | bytes 4194320 | tf_op jit(solution)/shard_map/all_gather | solution.py:92
  255.4 3.1 fusion
  258.5 74.5 %all-gather.5.cloned.1.call-done = bf16[4096,3,256]{0,2,1:T(8,128)(2,1)} async-done(((bf16[128,3,256]{0,2,1:T(8,128)(2,1)}), bf16[4096,3,256]{0,2,1:T(8,128)(2,1)}) %all-gather.5.cloned.1.call-update) | async-done | bytes 6291472 | tf_op jit(solution)/shard_map/all_gather | solution.py:58
  332.9 7.5 %fusion.29 = bf16[512,768]{1,0:T(8,128)(2,1)S(1)} fusion(bf16[4096,768]{0,1:T(8,128)(2,1)} %bitcast.160, bf16[512,4096]{1,0:T(8,128)(2,1)} %all-gather.3.cloned.1.call-done, f32[4096]{0:T(1024)S(1)} %copy-done.6, f32[512]{0:T(512)S(1)} %add_rsqrt_fusion), kind=kOutput, calls=%fused_computation.49 | convolution fusion | flops 3230007296 | bytes 11290624 | tf_op jit(solution)/shard_map/dot_general | solution.py:97
  340.5 3.2 collective-permute-start.7
  343.8 3.3 collective-permute-start.8
  349.9 2.8 collective-permute-done.7
  352.9 28.8 %collective-permute-done.8 = bf16[512,512]{1,0:T(8,128)(2,1)S(1)} collective-permute-done((bf16[512,512]{1,0:T(8,128)(2,1)S(1)}, bf16[512,512]{1,0:T(8,128)(2,1)S(1)}, u32[]{:S(2)}, u32[]{:S(2)}) %collective-permute-start.8) | collective-permute-done | bytes 524320 | tf_op jit(solution)/shard_map/ppermute | solution.py:23
  (74 shorter events, 43.3 us)
Async XLA Ops:
  7.2 248.2 %all-gather.3.cloned.1.call-start = ((), (), s32[]{:S(2)}) async-start(), calls=%async_computation | async-start | bytes 4718592 | tf_op jit(solution)/shard_map/all_gather | solution.py:92
  8.0 21.4 %collective-permute-start = (bf16[6,3,512]{2,0,1:T(8,128)(2,1)S(1)}, bf16[6,3,512]{2,0,1:T(8,128)(2,1)S(1)}, u32[]{:S(2)}, u32[]{:S(2)}) collective-permute-start(bf16[6,3,512]{2,0,1:T(8,128)(2,1)S(1)} %slice.102), channel_id=1, source_target_pairs={{0,8},{8,16},{16,24},{24,32},{32,40},{40,48},{48,56},{56,64},{64,7... | collective-permute-start | bytes 55304 | tf_op jit(solution)/shard_map/ppermute | solution.py:23
  23.5 5.8 %copy-start.2 = (bf16[512,3,512]{2,0,1:T(8,128)(2,1)S(1)}, bf16[512,3,512]{2,0,1:T(8,128)(2,1)}, u32[]{:S(2)}) copy-start(bf16[512,3,512]{2,0,1:T(8,128)(2,1)} %param.7) | copy-start | bytes 4718596
  80.0 10.5 %copy-start = (f32[16,512]{1,0:T(8,128)S(1)}, f32[16,512]{1,0:T(8,128)}, u32[]{:S(2)}) copy-start(f32[16,512]{1,0:T(8,128)} %param.9) | copy-start | bytes 98308
  91.1 3.1 collective-permute-start.1
  94.2 6.6 %collective-permute-start.2 = (f32[16,512]{1,0:T(8,128)S(1)}, f32[16,512]{1,0:T(8,128)S(1)}, u32[]{:S(2)}, u32[]{:S(2)}) collective-permute-start(f32[16,512]{1,0:T(8,128)S(1)} %collective-permute-done.1), channel_id=1, source_target_pairs={{0,8},{8,16},{16,24},{24,32},{32,40},{40,48},{48,56},{56,64},{64,7... | collective-permute-start | bytes 98312 | tf_op jit(solution)/shard_map/ppermute | solution.py:23
  100.9 8.2 %collective-permute-start.3 = (f32[16,512]{1,0:T(8,128)S(1)}, f32[16,512]{1,0:T(8,128)S(1)}, u32[]{:S(2)}, u32[]{:S(2)}) collective-permute-start(f32[16,512]{1,0:T(8,128)S(1)} %multiply_add_fusion.4), channel_id=1, source_target_pairs={{0,16},{8,24},{16,32},{24,40},{32,48},{40,56},{48,64},{56,72},{64,... | collective-permute-start | bytes 98312 | tf_op jit(solution)/shard_map/ppermute | solution.py:23
  109.0 8.0 %collective-permute-start.4 = (f32[16,512]{1,0:T(8,128)S(1)}, f32[16,512]{1,0:T(8,128)S(1)}, u32[]{:S(2)}, u32[]{:S(2)}) collective-permute-start(f32[16,512]{1,0:T(8,128)S(1)} %multiply_add_fusion.3), channel_id=1, source_target_pairs={{0,32},{8,40},{16,48},{24,56},{32,64},{40,72},{48,80},{56,88},{64,... | collective-permute-start | bytes 98312 | tf_op jit(solution)/shard_map/ppermute | solution.py:23
  117.0 9.8 %collective-permute-start.5 = (f32[16,512]{1,0:T(8,128)S(1)}, f32[16,512]{1,0:T(8,128)S(1)}, u32[]{:S(2)}, u32[]{:S(2)}) collective-permute-start(f32[16,512]{1,0:T(8,128)S(1)} %multiply_add_fusion.2), channel_id=1, source_target_pairs={{0,64},{8,72},{16,80},{24,88},{32,96},{40,104},{48,112},{56,120},{... | collective-permute-start | bytes 98312 | tf_op jit(solution)/shard_map/ppermute | solution.py:23
  126.8 8.3 %collective-permute-start.6 = (f32[16,512]{1,0:T(8,128)S(1)}, f32[16,512]{1,0:T(8,128)}, u32[]{:S(2)}, u32[]{:S(2)}) collective-permute-start(f32[16,512]{1,0:T(8,128)S(1)} %multiply_add_fusion.1), channel_id=1, source_target_pairs={{0,128},{8,136},{16,144},{24,152},{32,160},{40,168},{48,176},{56,1... | collective-permute-start | bytes 98312 | tf_op jit(solution)/shard_map/ppermute | solution.py:23
  139.6 10.0 %copy-start.5 = (f32[512]{0:T(512)S(1)}, f32[512]{0:T(512)}, u32[]{:S(2)}) copy-start(f32[512]{0:T(512)} %param.11) | copy-start | bytes 6148
  149.6 2.7 copy-start.4
  152.2 180.7 %copy-start.6 = (f32[4096]{0:T(1024)S(1)}, f32[4096]{0:T(1024)}, u32[]{:S(2)}) copy-start(f32[4096]{0:T(1024)} %param.12) | copy-start | bytes 49156
  152.2 180.7 %all-gather.5.cloned.1.call-start = ((), (), s32[]{:S(2)}) async-start(), calls=%async_computation.1 | async-start | bytes 6488064 | tf_op jit(solution)/shard_map/all_gather | solution.py:58
  340.5 12.2 %collective-permute-start.7 = (bf16[512,512]{1,0:T(8,128)(2,1)S(1)}, bf16[512,512]{1,0:T(8,128)(2,1)S(1)}, u32[]{:S(2)}, u32[]{:S(2)}) collective-permute-start(bf16[512,512]{1,0:T(8,128)(2,1)S(1)} %slice.148), channel_id=1, source_target_pairs={{0,8},{8,16},{16,24},{24,32},{32,40},{40,48},{48,56},{56,64},{64,7... | collective-permute-start | bytes 1572872 | tf_op jit(solution)/shard_map/ppermute | solution.py:23
  343.8 38.0 %collective-permute-start.8 = (bf16[512,512]{1,0:T(8,128)(2,1)S(1)}, bf16[512,512]{1,0:T(8,128)(2,1)S(1)}, u32[]{:S(2)}, u32[]{:S(2)}) collective-permute-start(bf16[512,512]{1,0:T(8,128)(2,1)S(1)} %slice.148), channel_id=1, source_target_pairs={{0,16},{8,24},{16,32},{24,40},{32,48},{40,56},{48,64},{56,72},{64,... | collective-permute-start | bytes 1572872 | tf_op jit(solution)/shard_map/ppermute | solution.py:23
  383.1 3.0 copy-start.1
  387.4 1.0 copy-start.3
Sparse Core Ops, SparseCore 0:
  152.4 102.9 all-gather.2
  258.4 74.4 all-gather.4
where the time goes:
time: 398 us; the launch traced here: 397 us
  waiting for transfers between devices  222 us (56%)
  local copies, waits for them, and re-layouts  44.1 us (11%)
  other arithmetic  43.3 us (11%)
  starting transfers between devices  37.1 us (9%)
  matrix products  35.9 us (9%)
  between operations  14.3 us (4%)
    all_gather x1, waiting for transfers between devices, on_device(): gathered = lax.all_gather(mixer, 'tp', axis=1, tiled=True)  102 us
    all_gather x1, waiting for transfers between devices, on_device(): shard_rows = lax.all_gather(qkv_weight, 'ctx', axis=0, tiled=True)  74.5 us
    ppermute x9, waiting for transfers between devices, from_behind(): lax.ppermute(value, axis, [(source, source + steps) for source in range(l...  45.3 us
    ppermute x9, starting transfers between devices, from_behind(): lax.ppermute(value, axis, [(source, source + steps) for source in range(l...  37 us
    reshape x1, local copies, waits for them, and re-layouts, local_modal_conv(): jnp.einsum('ts,qsk->qtk', tri, lifted, precision=PRECISE)  19.9 us
    dot_general x1, matrix products, local_modal_conv(): jnp.einsum('ts,qsk->qtk', tri, lifted, precision=PRECISE)  14.5 us
    reduce_sum x1, other arithmetic, local_modal_conv(): intra = jnp.sum(states * mixing[None, None], axis=2)  10.5 us
    mul x1, other arithmetic, local_modal_conv(): up[None] * blocks[:, :, None, :]  9.46 us
  transfers between devices with their start and end apart: 11, of which 9 were waited for; matrix products, arithmetic and copies ran while one was open for 7% of the time, Pallas kernels for 0%

commit v1 on v0

--- a/solution.py
+++ b/solution.py
@@ -89,7 +89,10 @@
     filtered = (intra + carried).reshape(tok_dev, channels) + skip_gain[None] * gated
     filtered = to_bf16_grid(filtered)
     mixer = (short_conv[:, 0] * filtered).astype(jnp.bfloat16)
-    gathered = lax.all_gather(mixer, "tp", axis=1, tiled=True)
+    local_out = lax.axis_size("tp")
+    now = jnp.stack(local_out * [mixer])
+    met_up = lax.all_to_all(now, split_axis=0, concat_axis=0, axis_name="tp")
+    gathered = jnp.concatenate(met_up, axis=1)
     as_float = gathered.astype(jnp.float32)
     inverse = lax.rsqrt(jnp.mean(as_float * as_float, axis=1, keepdims=True) + EPSILON)
     normed = (as_float * inverse * norm_gain[None]).astype(jnp.bfloat16)

time: 398 us -> 289 us (0.73)
  waiting for transfers between devices: 222 us -> 88.5 us
  starting transfers between devices: 37.1 us -> 48.1 us
  local copies, waits for them, and re-layouts: 44.1 us -> 53.2 us
  other arithmetic: 43.3 us -> 47.5 us
    all_gather x1 -> x0, waiting for transfers between devices: 102 us -> none  [on_device(): gathered = lax.all_gather(mixer, 'tp', axis=1, tiled=True)]
    all_gather x1, waiting for transfers between devices: 74.5 us -> 0.01 us  [on_device(): shard_rows = lax.all_gather(qkv_weight, 'ctx', axis=0, tiled=True)]
    all_to_all x0 -> x1, waiting for transfers between devices: none -> 37.2 us  [on_device(): met_up = lax.all_to_all(now, split_axis=0, concat_axis=0, axis_name='tp')]
    ppermute x9, waiting for transfers between devices: 45.3 us -> 51.3 us  [from_behind(): lax.ppermute(value, axis, [(source, source + steps) for source in range(l...]
    ppermute x9, starting transfers between devices: 37 us -> 42.7 us  [from_behind(): lax.ppermute(value, axis, [(source, source + steps) for source in range(l...]
    all_to_all x0 -> x1, starting transfers between devices: none -> 5.36 us  [on_device(): met_up = lax.all_to_all(now, split_axis=0, concat_axis=0, axis_name='tp')]
    convert_element_type x0 -> x1, other arithmetic: none -> 4.11 us  [on_device(): normed = (as_float * inverse * norm_gain[None]).astype(jnp.bfloat16)]
  transfers between devices with their start and end apart: 11 -> 11, of which waited for: 9 -> 8; matrix products, arithmetic and copies ran while one was open for 7% -> 41% of each run, Pallas kernels for 0% -> 0%
where the time goes in v1:
time: 289 us; the launch traced here: 284 us
  waiting for transfers between devices  88.5 us (31%)
  local copies, waits for them, and re-layouts  53.2 us (18%)
  starting transfers between devices  48.1 us (17%)
  other arithmetic  47.5 us (16%)
  matrix products  32.7 us (11%)
  between operations  14.3 us (5%)
    ppermute x9, waiting for transfers between devices, from_behind(): lax.ppermute(value, axis, [(source, source + steps) for source in range(l...  51.3 us
    ppermute x9, starting transfers between devices, from_behind(): lax.ppermute(value, axis, [(source, source + steps) for source in range(l...  42.7 us
    all_to_all x1, waiting for transfers between devices, on_device(): met_up = lax.all_to_all(now, split_axis=0, concat_axis=0, axis_name='tp')  37.2 us
    reshape x1, local copies, waits for them, and re-layouts, local_modal_conv(): jnp.einsum('ts,qsk->qtk', tri, lifted, precision=PRECISE)  20.1 us
    dot_general x1, matrix products, local_modal_conv(): jnp.einsum('ts,qsk->qtk', tri, lifted, precision=PRECISE)  14.5 us
    reduce_sum x1, other arithmetic, local_modal_conv(): intra = jnp.sum(states * mixing[None, None], axis=2)  10.6 us
    mul x1, other arithmetic, local_modal_conv(): up[None] * blocks[:, :, None, :]  9.47 us
    dot_general x1, matrix products, on_device(): jnp.dot(normed, flat_rows, preferred_element_type=jnp.float32)  7.52 us
  transfers between devices with their start and end apart: 11, of which 8 were waited for; matrix products, arithmetic and copies ran while one was open for 41% of the time, Pallas kernels for 0%

profile of v1, /device:TPU:105, one launch (start us, length us, event | category | flops | bytes accessed | tf_op | source)
XLA Modules:
  0.0 284.4 jit_solution(16225001903110963648)
XLA Ops:
  8.0 3.7 %collective-permute-start = (bf16[6,3,512]{2,0,1:T(8,128)(2,1)S(1)}, bf16[6,3,512]{2,0,1:T(8,128)(2,1)S(1)}, u32[]{:S(2)}, u32[]{:S(2)}) collective-permute-start(bf16[6,3,512]{2,0,1:T(8,128)(2,1)S(1)} %slice.102), channel_id=1, source_target_pairs={{0,8},{8,16},{16,24},{24,32},{32,40},{40,48},{48,56},{56,64},{64,7... | collective-permute-start | bytes 55304 | tf_op jit(solution)/shard_map/ppermute | solution.py:23
  17.1 4.6 %multiply_exponential_fusion = f32[128,8192]{0,1:T(8,128)} fusion(f32[8192]{0:T(1024)S(1)} %bitcast.163, f32[128]{0:T(128)S(1)} %iota_add_fusion), kind=kLoop, calls=%fused_computation.12 | loop fusion | flops 1048576 | bytes 4227584 | tf_op jit(solution)/shard_map/exp | solution.py:32
  21.7 3.5 %multiply_exponential_fusion.1 = f32[128,16,512]{0,1,2:T(8,128)} fusion(f32[16,512]{0,1:T(8,128)S(1)} %copy.51, f32[128]{0:T(128)S(1)} %fusion.81), kind=kLoop, calls=%fused_computation.13 | loop fusion | flops 1048576 | bytes 4227584 | tf_op jit(solution)/shard_map/exp | solution.py:33
  25.3 5.7 %copy.52 = f32[128,16,512]{2,1,0:T(8,128)} copy(f32[128,16,512]{0,1,2:T(8,128)} %multiply_exponential_fusion.1) | data formatting | bytes 8388608 | tf_op jit(solution)/shard_map/exp | solution.py:33
  37.9 9.5 %bitcast_multiply_fusion = f32[4,128,8192]{1,2,0:T(8,128)} fusion(f32[4,128,512]{1,2,0:T(8,128)} %copy.53, f32[128,8192]{0,1:T(8,128)} %multiply_exponential_fusion), kind=kLoop, calls=%fused_computation | loop fusion | flops 4194304 | bytes 22020096 | tf_op jit(solution)/shard_map/mul | solution.py:37
  47.4 14.5 %fusion.71 = f32[4,8192,128]{2,1,0:T(8,128)} fusion(f32[4,128,8192]{1,2,0:T(8,128)} %bitcast_multiply_fusion), kind=kOutput, calls=%fused_computation.99 | convolution fusion | flops 6442467328 | bytes 33554432 | tf_op jit(solution)/shard_map/ts,qsk->qtk/dot_general | solution.py:38
  61.8 20.1 %copy.54 = f32[4,128,16,512]{3,2,1,0:T(8,128)} copy(f32[4,128,16,512]{1,3,2,0:T(8,128)} %bitcast.155) | data formatting | bytes 33554432 | tf_op jit(solution)/shard_map/reshape | solution.py:38
  81.9 10.6 %multiply_reduce_fusion = (f32[4,128,512]{2,1,0:T(8,128)}, f32[4,128,16,512]{3,2,1,0:T(8,128)S(1)}) fusion(f32[16,512]{1,0:T(8,128)S(1)} %sqrt_multiply_fusion, f32[4,128,16,512]{3,2,1,0:T(8,128)} %copy.54, f32[128,16,512]{2,1,0:T(8,128)} %copy.52), kind=kLoop, calls=%fused_computation.1 | loop fusion | flops 12320768 | bytes 38830080 | tf_op jit(solution)/shard_map/reduce_sum | solution.py:42
  96.2 4.0 %collective-permute-start.2 = (f32[16,512]{1,0:T(8,128)S(1)}, f32[16,512]{1,0:T(8,128)S(1)}, u32[]{:S(2)}, u32[]{:S(2)}) collective-permute-start(f32[16,512]{1,0:T(8,128)S(1)} %collective-permute-done.1), channel_id=1, source_target_pairs={{0,8},{8,16},{16,24},{24,32},{32,40},{40,48},{48,56},{56,64},{64,7... | collective-permute-start | bytes 98312 | tf_op jit(solution)/shard_map/ppermute | solution.py:23
  100.3 2.7 collective-permute-done.2
  104.9 6.1 %collective-permute-done.3 = f32[16,512]{1,0:T(8,128)S(1)} collective-permute-done((f32[16,512]{1,0:T(8,128)S(1)}, f32[16,512]{1,0:T(8,128)S(1)}, u32[]{:S(2)}, u32[]{:S(2)}) %collective-permute-start.3) | collective-permute-done | bytes 32800 | tf_op jit(solution)/shard_map/ppermute | solution.py:23
  111.0 5.1 %collective-permute-start.4 = (f32[16,512]{1,0:T(8,128)S(1)}, f32[16,512]{1,0:T(8,128)S(1)}, u32[]{:S(2)}, u32[]{:S(2)}) collective-permute-start(f32[16,512]{1,0:T(8,128)S(1)} %multiply_add_fusion.3), channel_id=1, source_target_pairs={{0,32},{8,40},{16,48},{24,56},{32,64},{40,72},{48,80},{56,88},{64,... | collective-permute-start | bytes 98312 | tf_op jit(solution)/shard_map/ppermute | solution.py:23
  116.1 2.8 %collective-permute-done.4 = f32[16,512]{1,0:T(8,128)S(1)} collective-permute-done((f32[16,512]{1,0:T(8,128)S(1)}, f32[16,512]{1,0:T(8,128)S(1)}, u32[]{:S(2)}, u32[]{:S(2)}) %collective-permute-start.4) | collective-permute-done | bytes 32800 | tf_op jit(solution)/shard_map/ppermute | solution.py:23
  118.9 8.7 %collective-permute-start.5 = (f32[16,512]{1,0:T(8,128)S(1)}, f32[16,512]{1,0:T(8,128)S(1)}, u32[]{:S(2)}, u32[]{:S(2)}) collective-permute-start(f32[16,512]{1,0:T(8,128)S(1)} %multiply_add_fusion.2), channel_id=1, source_target_pairs={{0,64},{8,72},{16,80},{24,88},{32,96},{40,104},{48,112},{56,120},{... | collective-permute-start | bytes 98312 | tf_op jit(solution)/shard_map/ppermute | solution.py:23
  128.7 4.9 %collective-permute-start.6 = (f32[16,512]{1,0:T(8,128)S(1)}, f32[16,512]{1,0:T(8,128)}, u32[]{:S(2)}, u32[]{:S(2)}) collective-permute-start(f32[16,512]{1,0:T(8,128)S(1)} %multiply_add_fusion.1), channel_id=1, source_target_pairs={{0,128},{8,136},{16,144},{24,152},{32,160},{40,168},{48,176},{56,1... | collective-permute-start | bytes 98312 | tf_op jit(solution)/shard_map/ppermute | solution.py:23
  141.5 7.4 %fusion.28 = f32[4,128,512]{1,0,2:T(4,128)} fusion(f32[4,128,512]{1,0,2:T(4,128)} %copy.57, f32[4,16,512]{1,0,2:T(4,128)} %copy.56, f32[16,512]{0,1:T(8,128)} %copy.55, f32[128]{0:T(128)S(1)} %add_negate_fusion, f32[16,512]{0,1:T(8,128)S(1)} %copy.51), kind=kOutput, calls=%fused_computation.48 | convolution fusion | flops 52690944 | bytes 2294272 | tf_op jit(solution)/shard_map/lnc,qnc->qlc/dot_general | solution.py:88
  157.6 5.4 %all-to-all-start = ((bf16[8,512,512]{1,2,0:T(8,128)(2,1)}), bf16[8,512,512]{1,2,0:T(8,128)(2,1)}, u32[]{:S(2)}, u32[]{:S(2)}) async-start(bf16[8,512,512]{1,2,0:T(8,128)(2,1)} %stack.43), calls=%async_computation | async-start | bytes 8388608 | tf_op jit(solution)/shard_map/all_to_all | solution.py:94
  163.1 37.2 %all-to-all-done = bf16[8,512,512]{1,2,0:T(8,128)(2,1)} async-done(((bf16[8,512,512]{1,2,0:T(8,128)(2,1)}), bf16[8,512,512]{1,2,0:T(8,128)(2,1)}, u32[]{:S(2)}, u32[]{:S(2)}) %all-to-all-start) | async-done | bytes 4194336 | tf_op jit(solution)/shard_map/all_to_all | solution.py:94
  200.3 3.1 %fusion = f32[512]{0:T(512)S(1)} fusion(bf16[8,512,512]{1,2,0:T(8,128)(2,1)} %all-to-all-done), kind=kLoop, calls=%fused_computation.4 | loop fusion | flops 6290944 | bytes 4196352 | tf_op jit(solution)/shard_map/reduce_sum | solution.py:97
  203.4 4.1 %fusion.2 = bf16[8,512,512]{1,2,0:T(8,128)(2,1)} fusion(bf16[8,512,512]{1,2,0:T(8,128)(2,1)} %all-to-all-done, f32[8,512]{1,0:T(8,128)S(1)} %mul.344, f32[512]{0:T(512)S(1)} %add_rsqrt_fusion), kind=kLoop, calls=%fused_computation.6 | loop fusion | flops 8388608 | bytes 8407040 | tf_op jit(solution)/shard_map/convert_element_type | solution.py:98
  207.5 7.5 %convolution_convert_fusion = bf16[512,768]{1,0:T(8,128)(2,1)S(1)} fusion(bf16[512,4096]{0,1:T(8,128)(2,1)} %bitcast.156, bf16[4096,768]{0,1:T(8,128)(2,1)} %bitcast.165), kind=kOutput, calls=%fused_computation.46 | convolution fusion | flops 3221618688 | bytes 11272192 | tf_op jit(solution)/shard_map/dot_general | solution.py:100
  215.9 9.5 %collective-permute-start.7 = (bf16[512,512]{1,0:T(8,128)(2,1)}, bf16[512,512]{1,0:T(8,128)(2,1)}, u32[]{:S(2)}, u32[]{:S(2)}) collective-permute-start(bf16[512,512]{1,0:T(8,128)(2,1)} %slice.148), channel_id=1, source_target_pairs={{0,8},{8,16},{16,24},{24,32},{32,40},{40,48},{48,56},{56,64},{64,7... | collective-permute-start | bytes 1572872 | tf_op jit(solution)/shard_map/ppermute | solution.py:23
  225.4 2.7 collective-permute-start.8
  233.1 35.5 %collective-permute-done.8 = bf16[512,512]{1,0:T(8,128)(2,1)} collective-permute-done((bf16[512,512]{1,0:T(8,128)(2,1)}, bf16[512,512]{1,0:T(8,128)(2,1)}, u32[]{:S(2)}, u32[]{:S(2)}) %collective-permute-start.8) | collective-permute-done | bytes 524320 | tf_op jit(solution)/shard_map/ppermute | solution.py:23
  (75 shorter events, 51.1 us)
Async XLA Ops:
  7.2 200.4 %all-gather.2.cloned.1.call-start = ((), (), s32[]{:S(2)}) async-start(), calls=%async_computation.1 | async-start | bytes 6488064 | tf_op jit(solution)/shard_map/all_gather | solution.py:58
  8.0 23.1 %collective-permute-start = (bf16[6,3,512]{2,0,1:T(8,128)(2,1)S(1)}, bf16[6,3,512]{2,0,1:T(8,128)(2,1)S(1)}, u32[]{:S(2)}, u32[]{:S(2)}) collective-permute-start(bf16[6,3,512]{2,0,1:T(8,128)(2,1)S(1)} %slice.102), channel_id=1, source_target_pairs={{0,8},{8,16},{16,24},{24,32},{32,40},{40,48},{48,56},{56,64},{64,7... | collective-permute-start | bytes 55304 | tf_op jit(solution)/shard_map/ppermute | solution.py:23
  25.3 5.8 %copy-start.1 = (bf16[512,3,512]{2,0,1:T(8,128)(2,1)S(1)}, bf16[512,3,512]{2,0,1:T(8,128)(2,1)}, u32[]{:S(2)}) copy-start(bf16[512,3,512]{2,0,1:T(8,128)(2,1)} %param.7) | copy-start | bytes 4718596
  81.9 10.6 %copy-start = (f32[16,512]{1,0:T(8,128)S(1)}, f32[16,512]{1,0:T(8,128)}, u32[]{:S(2)}) copy-start(f32[16,512]{1,0:T(8,128)} %param.9) | copy-start | bytes 98308
  93.1 3.1 %collective-permute-start.1 = (f32[16,512]{1,0:T(8,128)S(1)}, f32[16,512]{1,0:T(8,128)S(1)}, u32[]{:S(2)}, u32[]{:S(2)}) collective-permute-start(f32[16,512]{1,0:T(8,128)S(1)} %get-tuple-element.13), channel_id=1, source_target_pairs={{0,8},{8,16},{16,24},{24,32},{32,40},{40,48},{48,56},{56,64},{64,7... | collective-permute-start | bytes 98312 | tf_op jit(solution)/shard_map/ppermute | solution.py:23
  96.2 6.7 %collective-permute-start.2 = (f32[16,512]{1,0:T(8,128)S(1)}, f32[16,512]{1,0:T(8,128)S(1)}, u32[]{:S(2)}, u32[]{:S(2)}) collective-permute-start(f32[16,512]{1,0:T(8,128)S(1)} %collective-permute-done.1), channel_id=1, source_target_pairs={{0,8},{8,16},{16,24},{24,32},{32,40},{40,48},{48,56},{56,64},{64,7... | collective-permute-start | bytes 98312 | tf_op jit(solution)/shard_map/ppermute | solution.py:23
  103.0 8.0 %collective-permute-start.3 = (f32[16,512]{1,0:T(8,128)S(1)}, f32[16,512]{1,0:T(8,128)S(1)}, u32[]{:S(2)}, u32[]{:S(2)}) collective-permute-start(f32[16,512]{1,0:T(8,128)S(1)} %multiply_add_fusion.4), channel_id=1, source_target_pairs={{0,16},{8,24},{16,32},{24,40},{32,48},{40,56},{48,64},{56,72},{64,... | collective-permute-start | bytes 98312 | tf_op jit(solution)/shard_map/ppermute | solution.py:23
  111.0 8.0 %collective-permute-start.4 = (f32[16,512]{1,0:T(8,128)S(1)}, f32[16,512]{1,0:T(8,128)S(1)}, u32[]{:S(2)}, u32[]{:S(2)}) collective-permute-start(f32[16,512]{1,0:T(8,128)S(1)} %multiply_add_fusion.3), channel_id=1, source_target_pairs={{0,32},{8,40},{16,48},{24,56},{32,64},{40,72},{48,80},{56,88},{64,... | collective-permute-start | bytes 98312 | tf_op jit(solution)/shard_map/ppermute | solution.py:23
  118.9 9.7 %collective-permute-start.5 = (f32[16,512]{1,0:T(8,128)S(1)}, f32[16,512]{1,0:T(8,128)S(1)}, u32[]{:S(2)}, u32[]{:S(2)}) collective-permute-start(f32[16,512]{1,0:T(8,128)S(1)} %multiply_add_fusion.2), channel_id=1, source_target_pairs={{0,64},{8,72},{16,80},{24,88},{32,96},{40,104},{48,112},{56,120},{... | collective-permute-start | bytes 98312 | tf_op jit(solution)/shard_map/ppermute | solution.py:23
  128.7 8.3 %collective-permute-start.6 = (f32[16,512]{1,0:T(8,128)S(1)}, f32[16,512]{1,0:T(8,128)}, u32[]{:S(2)}, u32[]{:S(2)}) collective-permute-start(f32[16,512]{1,0:T(8,128)S(1)} %multiply_add_fusion.1), channel_id=1, source_target_pairs={{0,128},{8,136},{16,144},{24,152},{32,160},{40,168},{48,176},{56,1... | collective-permute-start | bytes 98312 | tf_op jit(solution)/shard_map/ppermute | solution.py:23
  141.5 10.0 %copy-start.5 = (f32[512]{0:T(512)S(1)}, f32[512]{0:T(512)}, u32[]{:S(2)}) copy-start(f32[512]{0:T(512)} %param.11) | copy-start | bytes 6148
  157.6 5.4 %copy-start.4 = (f32[4096]{0:T(1024)S(1)}, f32[4096]{0:T(1024)}, u32[]{:S(2)}) copy-start(f32[4096]{0:T(1024)} %param.12) | copy-start | bytes 49156
  157.6 42.7 %all-to-all-start = ((bf16[8,512,512]{1,2,0:T(8,128)(2,1)}), bf16[8,512,512]{1,2,0:T(8,128)(2,1)}, u32[]{:S(2)}, u32[]{:S(2)}) async-start(bf16[8,512,512]{1,2,0:T(8,128)(2,1)} %stack.43), calls=%async_computation | async-start | bytes 8388608 | tf_op jit(solution)/shard_map/all_to_all | solution.py:94
  215.9 16.0 %collective-permute-start.7 = (bf16[512,512]{1,0:T(8,128)(2,1)}, bf16[512,512]{1,0:T(8,128)(2,1)}, u32[]{:S(2)}, u32[]{:S(2)}) collective-permute-start(bf16[512,512]{1,0:T(8,128)(2,1)} %slice.148), channel_id=1, source_target_pairs={{0,8},{8,16},{16,24},{24,32},{32,40},{40,48},{48,56},{56,64},{64,7... | collective-permute-start | bytes 1572872 | tf_op jit(solution)/shard_map/ppermute | solution.py:23
  225.4 43.2 %collective-permute-start.8 = (bf16[512,512]{1,0:T(8,128)(2,1)}, bf16[512,512]{1,0:T(8,128)(2,1)}, u32[]{:S(2)}, u32[]{:S(2)}) collective-permute-start(bf16[512,512]{1,0:T(8,128)(2,1)} %slice.148), channel_id=1, source_target_pairs={{0,16},{8,24},{16,32},{24,40},{32,48},{40,56},{48,64},{56,72},{64,... | collective-permute-start | bytes 1572872 | tf_op jit(solution)/shard_map/ppermute | solution.py:23
  272.2 0.9 copy-start.2
  275.2 1.0 copy-start.3
Sparse Core Ops, SparseCore 0:
  13.5 74.2 all-gather.1
